TPU v7x, 32 devices: a whole 2x2x4 slice. The times are simulated.
32 devices in a mesh: group: 2 (over y), member: 4 (over z), strip: 2 (over x), sub: 2 (over core).
Axes of the slice: x: 2, y: 2, z: 4, core: 2. Of those that a mesh axis runs over, the one named last changes fastest.
Arguments:
- noisy: bfloat16 [8, 128, 128, 256], P(('group', 'member'), None, 'strip', 'sub'), parts along dimension 0, may hold values from -6 to 6
- condition: bfloat16 [24, 128, 256], P('group', ('strip', 'member'), 'sub'), parts along dimension 0, may hold values from -6 to 6
- levels: int32 [8], P(('group', 'member')), parts along dimension 0, may hold values from 0 to 17
- enc_w1: bfloat16 [9, 128, 12], replicated, may hold values from -0.625 to 0.625
- enc_b1: float32 [128], replicated, may hold values from -4 to 4
- enc_w2: bfloat16 [9, 128, 128], replicated, may hold values from -0.1875 to 0.1875
- enc_b2: float32 [128], replicated, may hold values from -4 to 4
- den_wa: bfloat16 [9, 128, 256], replicated, may hold values from -0.125 to 0.125
- den_ba: float32 [128], replicated, may hold values from -4 to 4
- noise_gain: float32 [128], replicated, may hold values from -6 to 6
- den_wb: bfloat16 [9, 128, 128], replicated, may hold values from -0.1875 to 0.1875
Outputs:
- denoised: bfloat16 [8, 128, 128, 256], P(('group', 'member'), None, 'strip', 'sub'), parts along dimension 0
There are 2 independent parts, one for each index of `group`. A program takes and returns all parts, laid end to end along the dimension named above; an argument that names none is the same for every part. Nothing has to cross between parts.
All inputs are finite; a program needn't handle non-finite values.
Results may differ from a plain program's by a relative error of at most 0.0043.
The roundings to bfloat16 on the way count: a program that leaves them out, or rounds other values in their place, can miss the bound.
Values may be sent and summed in bfloat16 or wider, within the bound.
A program may use at most 64 MiB of HBM per device.

v0:
```python
import functools

import jax
import jax.numpy as jnp
from jax import lax
from jax.experimental import pallas as pl
from jax.experimental.pallas import tpu as pltpu
from jax.sharding import PartitionSpec as P

LEVELS = 18
SIGMA_DATA = 0.5
SIG_LOW = 0.25
SIG_HIGH = 4.0
SIDE = 8
DEEP = 4
NEAR = 2
CH = 16
MESH = pl.DeviceIdType.MESH
DIRS = [(a, b) for a in (-1, 0, 1) for b in (-1, 0, 1) if (a, b) != (0, 0)]


def exchange_kernel(
    members, strips, subs, cond_ref, noisy_ref, cond_out, rows_out, cols_out,
    own_sem, gather_send, gather_recv, cond_send, cond_recv, noisy_send, noisy_recv,
):
    member = lax.axis_index("member")
    strip = lax.axis_index("strip")
    sub = lax.axis_index("sub")
    share, _, width = cond_ref.shape
    rows = share * members
    cols = noisy_ref.shape[1]

    def beside(a, b):
        return {
            "strip": lax.rem(strip + a + strips, strips),
            "sub": lax.rem(sub + b + subs, subs),
        }

    mine = cond_out.at[pl.ds(DEEP + member * share, share), :, pl.ds(width, width)]
    own = pltpu.make_async_copy(cond_ref, mine, own_sem)
    own.start()

    barrier = pltpu.get_barrier_semaphore()
    for step in range(1, members):
        pl.semaphore_signal(
            barrier, inc=1, device_id={"member": lax.rem(member + step, members)},
            device_id_type=MESH,
        )
    for a, b in DIRS:
        pl.semaphore_signal(barrier, inc=1, device_id=beside(a, b), device_id_type=MESH)
    pl.semaphore_wait(barrier, members - 1 + len(DIRS))

    gathers = []
    for step in range(1, members):
        copy = pltpu.make_async_remote_copy(
            src_ref=cond_ref, dst_ref=mine,
            send_sem=gather_send.at[step], recv_sem=gather_recv.at[step],
            device_id={"member": lax.rem(member + step, members)}, device_id_type=MESH,
        )
        copy.start()
        gathers.append(copy)

    fields = []
    for at, (a, b) in enumerate(DIRS):
        src_col = 0 if b < 0 else (cols - SIDE if b > 0 else 0)
        dst_col = SIDE + cols if b < 0 else (0 if b > 0 else SIDE)
        col_n = SIDE if b else cols
        if a == 0:
            src = noisy_ref.at[:, pl.ds(src_col, SIDE), :]
            dst = cols_out.at[1 if b < 0 else 0]
        else:
            src = noisy_ref.at[pl.ds(0 if a < 0 else rows - NEAR, NEAR), pl.ds(src_col, col_n), :]
            dst = rows_out.at[1 if a < 0 else 0, :, pl.ds(dst_col, col_n), :]
        copy = pltpu.make_async_remote_copy(
            src_ref=src, dst_ref=dst, send_sem=noisy_send.at[at], recv_sem=noisy_recv.at[at],
            device_id=beside(a, b), device_id_type=MESH,
        )
        copy.start()
        fields.append(copy)

    own.wait()
    for copy in gathers:
        copy.wait()
    conds = []
    for at, (a, b) in enumerate(DIRS):
        dst_lane = 2 * width if b < 0 else (0 if b > 0 else width)
        if a == 0:
            src_row, dst_row, row_n = DEEP, DEEP, rows
        else:
            src_row = DEEP if a < 0 else rows
            dst_row = DEEP + rows if a < 0 else 0
            row_n = DEEP
        copy = pltpu.make_async_remote_copy(
            src_ref=cond_out.at[pl.ds(src_row, row_n), :, pl.ds(width, width)],
            dst_ref=cond_out.at[pl.ds(dst_row, row_n), :, pl.ds(dst_lane, width)],
            send_sem=cond_send.at[at], recv_sem=cond_recv.at[at],
            device_id=beside(a, b), device_id_type=MESH,
        )
        copy.start()
        conds.append(copy)
    for copy in fields + conds:
        copy.wait()


def exchange(cond, noisy, members, strips, subs):
    share, _, width = cond.shape
    rows, cols, chans = noisy.shape
    dma = pltpu.SemaphoreType.DMA
    vmem = pl.BlockSpec(memory_space=pltpu.VMEM)
    return pl.pallas_call(
        functools.partial(exchange_kernel, members, strips, subs),
        out_shape=(
            jax.ShapeDtypeStruct((rows + 2 * DEEP, CH, 3 * width), jnp.bfloat16),
            jax.ShapeDtypeStruct((2, NEAR, cols + 2 * SIDE, chans), jnp.bfloat16),
            jax.ShapeDtypeStruct((2, rows, SIDE, chans), jnp.bfloat16),
        ),
        in_specs=[vmem, pl.BlockSpec(memory_space=pl.ANY)],
        out_specs=(vmem, vmem, vmem),
        scratch_shapes=[
            dma, dma((members,)), dma((members,)), dma((8,)), dma((8,)), dma((8,)), dma((8,)),
        ],
        compiler_params=pltpu.CompilerParams(collective_id=0, has_side_effects=True),
        name="exchange",
    )(cond, noisy)


def largest_part(count, most):
    return max(n for n in range(1, most + 1) if count % n == 0)


NT = (((1,), (1,)), ((), ()))
TN = (((0,), (1,)), ((), ()))


def network_kernel(
    bounds, scales, cond_ref, noisy_ref, rows_ref, cols_ref, w1_ref, w2_ref, wa_ref, wb_ref,
    b1_ref, b2_ref, ba_ref, out_ref, first, feats, field, hidden, k2, kn, kf, kb,
):
    rows, cols, chans = noisy_ref.shape
    span = cols + 2 * SIDE
    wide = 3 * chans

    def place(dst, src, start):
        dst[...] = jnp.zeros_like(dst)
        for out_row in range(2):
            for a in range(3):
                side, spot = divmod(out_row + a, 2)
                for b in range(3):
                    dst[side, out_row * chans:(out_row + 1) * chans,
                        spot * wide + b * chans:spot * wide + (b + 1) * chans] = (
                        src[3 * a + b, :, start:start + chans])

    place(k2, w2_ref, 0)
    place(kn, wa_ref, 0)
    place(kf, wa_ref, chans)
    place(kb, wb_ref, 0)

    col_at = lax.broadcasted_iota(jnp.int32, (span, chans), 0)
    inside_cols = (col_at >= bounds[2]) & (col_at < bounds[3])

    def masked(values, row):
        keep = inside_cols & (row >= bounds[0]) & (row < bounds[1])
        return jnp.where(keep, values, 0.0)

    def keep_shifted(dst, pair, spot, values):
        base = spot * wide
        dst[pair, :, base:base + chans] = pltpu.roll(values, 1, 0).astype(jnp.bfloat16)
        dst[pair, :, base + chans:base + 2 * chans] = values.astype(jnp.bfloat16)
        dst[pair, :, base + 2 * chans:base + wide] = pltpu.roll(values, span - 1, 0).astype(jnp.bfloat16)

    def silu(v):
        return v / (1.0 + jnp.exp(-v))

    def stage(pairs, most, product, finish):
        part = largest_part(pairs, most)

        def body(step, carry):
            start = step * part
            result = product(start, part)
            for p in range(part):
                for spot in range(2):
                    finish(start + p, spot,
                           result[p * span:(p + 1) * span, spot * chans:(spot + 1) * chans])
            return carry

        lax.fori_loop(0, pairs // part, body, 0)

    def conv(source, weight, start, part):
        low = source[pl.ds(start, part)].reshape(part * span, 2 * wide)
        high = source[pl.ds(start + 1, part)].reshape(part * span, 2 * wide)
        return (lax.dot_general(low, weight[0], NT, preferred_element_type=jnp.float32)
                + lax.dot_general(high, weight[1], NT, preferred_element_type=jnp.float32))

    half = rows // 2

    width3 = cond_ref.shape[2]
    b1 = b1_ref[...]
    lane_at = lax.broadcasted_iota(jnp.int32, (4 * CH, width3), 1) - (width3 // 3 - SIDE)
    inside_lanes = (lane_at >= bounds[2]) & (lane_at < bounds[3])
    line_at = lax.broadcasted_iota(jnp.int32, (4 * CH, width3), 0)

    def first_product(start, part):
        pieces = []
        for p in range(part):
            block = cond_ref[pl.ds(2 * (start + p), 4)].reshape(4 * CH, width3).astype(jnp.float32)
            top = 2 * (start + p) - DEEP
            keep = (inside_lanes & (line_at >= (bounds[0] - top) * CH)
                    & (line_at < (bounds[1] - top) * CH))
            block = jnp.where(keep, block, 0.0)
            shifted = [
                pltpu.roll(block, width3 - (cols - SIDE + b - 1), 1)[:, :span].astype(jnp.bfloat16)
                for b in range(3)
            ]
            left = jnp.concatenate(shifted, axis=0)
            pieces.append(lax.dot_general(left, w1_ref[...], TN, preferred_element_type=jnp.float32))
        return jnp.concatenate(pieces, axis=0) if part > 1 else pieces[0]

    def first_finish(pair, spot, values):
        keep_shifted(first, pair, spot, masked(silu(values + b1), 2 * pair + spot - 3))

    stage(half + 3, 1, first_product, first_finish)

    b2 = b2_ref[...]

    def feats_finish(pair, spot, values):
        keep_shifted(feats, pair, spot, masked(values + b2, 2 * pair + spot - 2))

    stage(half + 2, 2, lambda s, n: conv(first, k2, s, n), feats_finish)

    def scaled(values, row):
        return masked(scales[0] * values.astype(jnp.float32), row)

    for end in range(2):
        for r in range(NEAR):
            row = -NEAR + r if end == 0 else rows + r
            keep_shifted(field, (row + NEAR) // 2, (row + NEAR) % 2, scaled(rows_ref[end, r], row))

    def field_body(pair, carry):
        for spot in range(2):
            row = 2 * pair + spot
            values = jnp.concatenate(
                [cols_ref[0, row].astype(jnp.float32), noisy_ref[row].astype(jnp.float32),
                 cols_ref[1, row].astype(jnp.float32)], axis=0)
            keep_shifted(field, pair + 1, spot, scaled(values, row))
        return carry

    lax.fori_loop(0, half, field_body, 0)

    ba = ba_ref[...]

    def hidden_finish(pair, spot, values):
        keep_shifted(hidden, pair, spot, masked(silu(values + ba), 2 * pair + spot - 1))

    stage(half + 1, 3, lambda s, n: conv(field, kn, s, n) + conv(feats, kf, s, n), hidden_finish)

    def out_finish(pair, spot, values):
        row = 2 * pair + spot
        kept = scales[1] * noisy_ref[row].astype(jnp.float32)
        out_ref[row] = (kept + scales[2] * values[SIDE:SIDE + cols]).astype(jnp.bfloat16)

    stage(half, 2, lambda s, n: conv(hidden, kb, s, n), out_finish)


def network(bounds, scales, cond, noisy, row_ends, col_ends, w1, w2, wa, wb, b1, b2, ba):
    rows, cols, chans = noisy.shape
    span = cols + 2 * SIDE
    half = rows // 2
    vmem = pl.BlockSpec(memory_space=pltpu.VMEM)
    smem = pl.BlockSpec(memory_space=pltpu.SMEM)

    def held(pairs):
        return pltpu.VMEM((pairs, span, 6 * chans), jnp.bfloat16)

    return pl.pallas_call(
        network_kernel,
        out_shape=jax.ShapeDtypeStruct((rows, cols, chans), jnp.bfloat16),
        in_specs=[smem, smem] + [vmem] * 11,
        out_specs=vmem,
        scratch_shapes=[held(half + 3), held(half + 2), held(half + 2), held(half + 1)]
        + [pltpu.VMEM((2, 2 * chans, 6 * chans), jnp.bfloat16)] * 4,
        compiler_params=pltpu.CompilerParams(vmem_limit_bytes=60 * 1024 * 1024),
        name="network",
    )(bounds, scales, cond, noisy, row_ends, col_ends, w1, w2, wa, wb, b1, b2, ba)


def local(
    members, strips, subs,
    noisy, condition, levels, enc_w1, enc_b1, enc_w2, enc_b2, den_wa, den_ba, noise_gain, den_wb
):
    field = jnp.transpose(noisy[0], (1, 2, 0))
    rows, cols, chans = field.shape
    inputs = condition.shape[0]
    cond = jnp.pad(jnp.transpose(condition, (1, 0, 2)), ((0, 0), (0, CH - inputs), (0, 0)))
    cond_all, row_ends, col_ends = exchange(cond, field, members, strips, subs)

    level_value = levels[0].astype(jnp.float32)
    noise_sigma = SIG_LOW * (SIG_HIGH / SIG_LOW) ** (level_value / (LEVELS - 1))
    spread = noise_sigma * noise_sigma + SIGMA_DATA * SIGMA_DATA
    c_in = 1.0 / jnp.sqrt(spread)
    c_skip = SIGMA_DATA * SIGMA_DATA / spread
    c_out = noise_sigma * SIGMA_DATA / jnp.sqrt(spread)
    c_noise = jnp.log(noise_sigma) / 4.0
    scales = jnp.stack([c_in, c_skip, c_out])
    offset_a = (den_ba + c_noise * noise_gain)[None]

    strip = lax.axis_index("strip")
    sub = lax.axis_index("sub")
    bounds = jnp.stack([
        -strip * rows, (strips - strip) * rows,
        SIDE - sub * cols, SIDE + (subs - sub) * cols,
    ]).astype(jnp.int32)

    w1 = jnp.pad(enc_w1, ((0, 0), (0, 0), (0, CH - inputs))).reshape(3, 3, chans, CH)
    w1 = jnp.transpose(w1, (2, 1, 0, 3))
    w1 = jnp.concatenate([
        jnp.pad(w1, ((0, 0), (0, 0), (0, 1), (0, 0))),
        jnp.pad(w1, ((0, 0), (0, 0), (1, 0), (0, 0))),
    ], axis=0).reshape(2 * chans, 12 * CH)

    out = network(bounds, scales, cond_all, field, row_ends, col_ends, w1, enc_w2, den_wa, den_wb,
                  enc_b1[None], enc_b2[None], offset_a)
    return jnp.transpose(out, (2, 0, 1))[None]


def solution(mesh):
    return jax.shard_map(
        functools.partial(local, mesh.shape["member"], mesh.shape["strip"], mesh.shape["sub"]),
        mesh=mesh,
        in_specs=(
            P(("group", "member"), None, "strip", "sub"),
            P("group", ("strip", "member"), "sub"),
            P(("group", "member")),
            P(), P(), P(), P(), P(), P(), P(), P(),
        ),
        out_specs=P(("group", "member"), None, "strip", "sub"),
        check_vma=False,
    )
```

profile of v0, /device:TPU:0, one launch (start us, length us, event | category | flops | bytes accessed | tf_op | source)
XLA Modules:
  0.0 78.1 jit_solution(12784039605508578916)
XLA Ops:
  0.9 0.6 pad_add_fusion.bounds
  1.5 0.6 pad_maximum_fusion.scales
  2.0 1.2 %add_bitcast_fusion.ba_ref = f32[1,128]{1,0:T(1,128)} fusion(f32[128]{0:T(128)} %param.19, f32[128]{0:T(128)} %param.20, f32[]{:T(128)} %bitcast.13), kind=kLoop, calls=%fused_computation.8 | loop fusion | flops 256 | bytes 1540 | tf_op jit(solution)/shard_map/broadcast_in_dim | solution.py:304
  3.2 0.8 pad.17
  4.0 0.8 copy.23.w1_ref
  4.8 0.8 %copy.26 = bf16[12,16,128]{2,0,1:T(8,128)(2,1)S(1)} copy(bf16[12,16,128]{2,1,0:T(8,128)(2,1)} %param.12) | data formatting | bytes 98304 | tf_op args[1]
  5.6 0.6 pad.16.cond_ref
  6.2 4.2 %copy.21 = bf16[1,128,64,128]{1,3,2,0:T(8,128)(2,1)} copy(bf16[1,128,64,128]{3,2,1,0:T(8,128)(2,1)} %param.11) | data formatting | bytes 4194304 | tf_op args[0]
  10.4 17.2 %exchange.1 = (bf16[72,16,384]{2,1,0:T(8,128)(2,1)}, bf16[2,2,144,128]{3,2,1,0:T(8,128)(2,1)}, bf16[2,64,8,128]{3,2,1,0:T(8,128)(2,1)}) custom-call(bf16[16,16,128]{2,1,0:T(8,128)(2,1)} %pad.16.cond_ref, bf16[64,128,128]{2,1,0:T(8,128)(2,1)} %bitcast.22), custom_call_target="tpu_custom_call" | custom-call | tf_op jit(solution)/shard_map/exchange/pallas_call | solution.py:110
  27.6 46.4 %network.1 = bf16[64,128,128]{2,1,0:T(8,128)(2,1)} custom-call(s32[4]{0:T(128)} %pad_add_fusion.bounds, f32[3]{0:T(128)} %pad_maximum_fusion.scales, bf16[72,16,384]{2,1,0:T(8,128)(2,1)} %get-tuple-element.8.cond_ref, bf16[64,128,128]{2,1,0:T(8,128)(2,1)} %bitcast.23, bf16[2,2,144,128]{3,2,1,0:T(8,128)(2,1)} %get-tuple-element.9.rows_ref, ...), custom_call_target="tpu_custom_call" | custom-call | tf_op jit(solution)/shard_map/network/pallas_call | solution.py:274
  74.0 4.1 %copy.24 = bf16[1,128,64,128]{3,2,1,0:T(8,128)(2,1)} copy(bf16[1,128,64,128]{1,3,2,0:T(8,128)(2,1)} %bitcast.24) | data formatting | bytes 4194304 | tf_op jit(solution)/shard_map/broadcast_in_dim | solution.py:322
  (2 shorter events, 0.0 us)
where the time goes:
time: 78.5 us; the launch traced here: 78.1 us
  Pallas kernels  63.6 us (81%)
  local copies, waits for them, and re-layouts  11.3 us (14%)
  other arithmetic  2.3 us (3%)
  between operations  0.94 us (1%)
    pallas_call x1, Pallas kernels, network(): pl.pallas_call(network_kernel, out_shape=jax.ShapeDtypeStruct((rows, cols...  46.4 us
    pallas_call x1, Pallas kernels, exchange(): pl.pallas_call(functools.partial(exchange_kernel, members, strips, subs),...  17.2 us
    unnamed x2, local copies, waits for them, and re-layouts  4.99 us
    broadcast_in_dim x1, local copies, waits for them, and re-layouts, local(): return jnp.transpose(out, (2, 0, 1))[None]  4.11 us

commit v1 on v0

v1 whole, which is shorter than its diff:
```python
import functools
import math

import jax
import jax.numpy as jnp
from jax import lax
from jax.experimental import pallas as pl
from jax.experimental.pallas import tpu as pltpu
from jax.sharding import PartitionSpec as P

LEVELS = 18
SIGMA_DATA = 0.5
SIG_LOW = 0.25
SIG_HIGH = 4.0
SIDE = 8
DEEP = 4
NEAR = 2
CH = 16
MESH = pl.DeviceIdType.MESH
DIRS = [(a, b) for a in (-1, 0, 1) for b in (-1, 0, 1) if (a, b) != (0, 0)]


def exchange_kernel(
    members, strips, subs, cond_ref, noisy_ref, cond_out, rows_out, cols_out,
    own_sem, gather_send, gather_recv, cond_send, cond_recv, noisy_send, noisy_recv,
):
    member = lax.axis_index("member")
    strip = lax.axis_index("strip")
    sub = lax.axis_index("sub")
    share, _, width = cond_ref.shape
    rows = share * members
    cols = noisy_ref.shape[1]

    def exists(a, b):
        held = (strip + a >= 0) & (strip + a < strips)
        return held & (sub + b >= 0) & (sub + b < subs)

    def beside(a, b):
        return {
            "strip": lax.rem(strip + a + strips, strips),
            "sub": lax.rem(sub + b + subs, subs),
        }

    mine = cond_out.at[pl.ds(DEEP + member * share, share), :, pl.ds(width, width)]
    own = pltpu.make_async_copy(cond_ref, mine, own_sem)
    own.start()

    barrier = pltpu.get_barrier_semaphore()
    for step in range(1, members):
        pl.semaphore_signal(
            barrier, inc=1, device_id={"member": lax.rem(member + step, members)},
            device_id_type=MESH,
        )
    for a, b in DIRS:
        pl.semaphore_signal(barrier, inc=1, device_id=beside(a, b), device_id_type=MESH)
    pl.semaphore_wait(barrier, members - 1 + len(DIRS))

    gathers = []
    for step in range(1, members):
        copy = pltpu.make_async_remote_copy(
            src_ref=cond_ref, dst_ref=mine,
            send_sem=gather_send.at[step], recv_sem=gather_recv.at[step],
            device_id={"member": lax.rem(member + step, members)}, device_id_type=MESH,
        )
        copy.start()
        gathers.append(copy)

    def start_if_there(copies, at, a, b, **refs):
        copy = pltpu.make_async_remote_copy(
            device_id=beside(a, b), device_id_type=MESH, **refs)

        @pl.when(exists(a, b))
        def _():
            copy.start()

        copies.append((copy, a, b))

    fields = []
    for at, (a, b) in enumerate(DIRS):
        src_col = cols - SIDE if b > 0 else 0
        dst_col = SIDE + cols if b < 0 else (0 if b > 0 else SIDE)
        col_n = SIDE if b else cols
        if a == 0:
            src = noisy_ref.at[:, pl.ds(src_col, SIDE), :]
            dst = cols_out.at[1 if b < 0 else 0]
        else:
            src = noisy_ref.at[pl.ds(0 if a < 0 else rows - NEAR, NEAR), pl.ds(src_col, col_n), :]
            dst = rows_out.at[1 if a < 0 else 0, :, pl.ds(dst_col, col_n), :]
        start_if_there(fields, at, a, b, src_ref=src, dst_ref=dst,
                       send_sem=noisy_send.at[at], recv_sem=noisy_recv.at[at])

    own.wait()
    for copy in gathers:
        copy.wait()
    conds = []
    for at, (a, b) in enumerate(DIRS):
        dst_lane = 2 * width if b < 0 else (0 if b > 0 else width)
        if a == 0:
            src_row, dst_row, row_n = DEEP, DEEP, rows
        else:
            src_row = DEEP if a < 0 else rows
            dst_row = DEEP + rows if a < 0 else 0
            row_n = DEEP
        start_if_there(
            conds, at, a, b,
            src_ref=cond_out.at[pl.ds(src_row, row_n), :, pl.ds(width, width)],
            dst_ref=cond_out.at[pl.ds(dst_row, row_n), :, pl.ds(dst_lane, width)],
            send_sem=cond_send.at[at], recv_sem=cond_recv.at[at])
    for copy, a, b in fields + conds:
        @pl.when(exists(a, b))
        def _(copy=copy):
            copy.wait_send()

        @pl.when(exists(-a, -b))
        def _(copy=copy):
            copy.wait_recv()


def exchange(cond, noisy, members, strips, subs):
    share, _, width = cond.shape
    rows, cols, chans = noisy.shape
    dma = pltpu.SemaphoreType.DMA
    vmem = pl.BlockSpec(memory_space=pltpu.VMEM)
    return pl.pallas_call(
        functools.partial(exchange_kernel, members, strips, subs),
        out_shape=(
            jax.ShapeDtypeStruct((rows + 2 * DEEP, CH, 3 * width), jnp.bfloat16),
            jax.ShapeDtypeStruct((2, NEAR, cols + 2 * SIDE, chans), jnp.bfloat16),
            jax.ShapeDtypeStruct((2, rows, SIDE, chans), jnp.bfloat16),
        ),
        in_specs=[vmem, pl.BlockSpec(memory_space=pl.ANY)],
        out_specs=(vmem, vmem, vmem),
        scratch_shapes=[
            dma, dma((members,)), dma((members,)), dma((8,)), dma((8,)), dma((8,)), dma((8,)),
        ],
        compiler_params=pltpu.CompilerParams(collective_id=0, has_side_effects=True),
        name="exchange",
    )(cond, noisy)


def largest_part(count, most):
    return max(n for n in range(1, most + 1) if count % n == 0)


NT = (((1,), (1,)), ((), ()))
TN = (((0,), (1,)), ((), ()))


def network_kernel(
    strips, subs, levels, cond_ref, noisy_ref, rows_ref, cols_ref, w1_ref, w2_ref, wa_ref, wb_ref,
    b1_ref, b2_ref, ba_ref, gain_ref, out_ref, lines, first, feats, field, hidden, k2, kn, kf, kb,
):
    rows, cols, chans = noisy_ref.shape
    span = cols + 2 * SIDE
    wide = 3 * chans
    half = rows // 2
    strip = lax.axis_index("strip")
    sub = lax.axis_index("sub")
    row_low, row_high = -strip * rows, (strips - strip) * rows
    col_low, col_high = SIDE - sub * cols, SIDE + (subs - sub) * cols

    level = jnp.full((1, chans), levels[0], jnp.int32).astype(jnp.float32)
    sigma = SIG_LOW * jnp.exp(level / (LEVELS - 1) * math.log(SIG_HIGH / SIG_LOW))
    spread = sigma * sigma + SIGMA_DATA * SIGMA_DATA
    c_in = 1.0 / jnp.sqrt(spread)
    c_skip = SIGMA_DATA * SIGMA_DATA / spread
    c_out = sigma * SIGMA_DATA / jnp.sqrt(spread)
    c_noise = jnp.log(sigma) / 4.0
    b1 = b1_ref[...]
    b2 = b2_ref[...]
    ba = ba_ref[...] + c_noise * gain_ref[...]

    def place(dst, src, start):
        for out_row in range(2):
            dst[1 - out_row, out_row * chans:(out_row + 1) * chans,
                (1 - out_row) * wide:(2 - out_row) * wide] = jnp.zeros((chans, wide), jnp.bfloat16)
            for a in range(3):
                side, spot = divmod(out_row + a, 2)
                for b in range(3):
                    dst[side, out_row * chans:(out_row + 1) * chans,
                        spot * wide + b * chans:spot * wide + (b + 1) * chans] = (
                        src[3 * a + b, :, start:start + chans])

    place(k2, w2_ref, 0)
    place(kn, wa_ref, 0)
    place(kf, wa_ref, chans)
    place(kb, wb_ref, 0)

    col_at = lax.broadcasted_iota(jnp.int32, (span, chans), 0)
    inside_cols = (col_at >= col_low) & (col_at < col_high)

    def masked(values, row):
        keep = (row >= row_low) & (row < row_high)
        left = jnp.where(inside_cols[:SIDE] & keep, values[:SIDE], 0.0)
        right = jnp.where(inside_cols[SIDE + cols:] & keep, values[SIDE + cols:], 0.0)
        middle = jnp.where(keep, values[SIDE:SIDE + cols], 0.0)
        return jnp.concatenate([left, middle, right], axis=0)

    def keep_shifted(dst, pair, spot, values):
        base = spot * wide
        dst[pair, :, base:base + chans] = pltpu.roll(values, 1, 0).astype(jnp.bfloat16)
        dst[pair, :, base + chans:base + 2 * chans] = values.astype(jnp.bfloat16)
        dst[pair, :, base + 2 * chans:base + wide] = pltpu.roll(values, span - 1, 0).astype(jnp.bfloat16)

    def silu(v):
        h = 0.5 * v
        return h * jnp.tanh(h) + h

    def conv(source, weight, pair, part, low, high):
        left = source[pl.ds(pair, part), low:high].reshape(part * (high - low), 2 * wide)
        right = source[pl.ds(pair + 1, part), low:high].reshape(part * (high - low), 2 * wide)
        return (lax.dot_general(left, weight[0], NT, preferred_element_type=jnp.float32)
                + lax.dot_general(right, weight[1], NT, preferred_element_type=jnp.float32))

    def rows_of(result, part):
        height = result.shape[0] // part
        for p in range(part):
            for spot in range(2):
                yield p, spot, result[p * height:(p + 1) * height, spot * chans:(spot + 1) * chans]

    def run(count, most, *stages):
        part = largest_part(count, most)

        def body(step, carry):
            for stage in stages:
                stage(step * part, part)
            return carry

        lax.fori_loop(0, count // part, body, 0)

    width3 = cond_ref.shape[2]
    lane_at = lax.broadcasted_iota(jnp.int32, (2 * CH, width3), 1) - (width3 // 3 - SIDE)
    inside_lanes = (lane_at >= col_low) & (lane_at < col_high)

    def lines_stage(pair):
        row = 2 * pair - DEEP
        keep = inside_lanes & (row >= row_low) & (row < row_high)
        block = cond_ref[pl.ds(2 * pair, 2)].reshape(2 * CH, width3).astype(jnp.float32)
        block = jnp.where(keep, block, 0.0)
        for b in range(3):
            moved = pltpu.roll(block, width3 - (cols - SIDE + b - 1), 1)[:, :2 * chans]
            lines[pair, 2 * CH * b:2 * CH * (b + 1)] = moved.astype(jnp.bfloat16)

    def first_stage(pair):
        left = jnp.concatenate([lines[pair], lines[pair + 1]], axis=0)[:, :span]
        result = lax.dot_general(left, w1_ref[...], TN, preferred_element_type=jnp.float32)
        for spot in range(2):
            values = silu(result[:, spot * chans:(spot + 1) * chans] + b1)
            keep_shifted(first, pair, spot, masked(values, 2 * pair + spot - 3))

    def feats_stage(pair, part):
        result = conv(first, k2, pair, part, 0, span)
        for p, spot, values in rows_of(result, part):
            row = 2 * (pair + p) + spot - 2
            keep_shifted(feats, pair + p, spot, masked(values + b2, row))

    def scaled(values, row):
        return masked(c_in * values.astype(jnp.float32), row)

    for end in range(2):
        for r in range(NEAR):
            row = -NEAR + r if end == 0 else rows + r
            keep_shifted(field, (row + NEAR) // 2, (row + NEAR) % 2, scaled(rows_ref[end, r], row))

    def field_stage(pair):
        for spot in range(2):
            row = 2 * pair + spot - NEAR
            values = jnp.concatenate(
                [cols_ref[0, row].astype(jnp.float32), noisy_ref[row].astype(jnp.float32),
                 cols_ref[1, row].astype(jnp.float32)], axis=0)
            keep_shifted(field, pair, spot, scaled(values, row))

    def hidden_stage(pair, part):
        result = conv(field, kn, pair, part, 0, span) + conv(feats, kf, pair, part, 0, span)
        for p, spot, values in rows_of(result, part):
            row = 2 * (pair + p) + spot - 1
            keep_shifted(hidden, pair + p, spot, masked(silu(values + ba), row))

    def out_stage(pair, part):
        result = conv(hidden, kb, pair, part, SIDE, SIDE + cols)
        for p, spot, values in rows_of(result, part):
            row = 2 * (pair + p) + spot
            kept = c_skip * noisy_ref[row].astype(jnp.float32)
            out_ref[row] = (kept + c_out * values).astype(jnp.bfloat16)

    def each(stage):
        def several(pair, part):
            for p in range(part):
                stage(pair + p)
        return several

    run(half + DEEP, 4, each(lines_stage))
    run(half + 3, 5, each(first_stage))
    run(half + 2, 2, feats_stage)
    run(half, 4, lambda pair, part: each(field_stage)(pair + 1, part))
    run(half + 1, 3, hidden_stage)
    run(half, 4, out_stage)


def network(strips, subs, levels, cond, noisy, row_ends, col_ends, w1, w2, wa, wb, b1, b2, ba, gain):
    rows, cols, chans = noisy.shape
    span = cols + 2 * SIDE
    half = rows // 2
    vmem = pl.BlockSpec(memory_space=pltpu.VMEM)
    smem = pl.BlockSpec(memory_space=pltpu.SMEM)

    def held(pairs):
        return pltpu.VMEM((pairs, span, 6 * chans), jnp.bfloat16)

    return pl.pallas_call(
        functools.partial(network_kernel, strips, subs),
        out_shape=jax.ShapeDtypeStruct((rows, cols, chans), jnp.bfloat16),
        in_specs=[smem] + [vmem] * 12,
        out_specs=vmem,
        scratch_shapes=[pltpu.VMEM((half + DEEP, 6 * CH, 2 * chans), jnp.bfloat16)]
        + [held(half + 3), held(half + 2), held(half + 2), held(half + 1)]
        + [pltpu.VMEM((2, 2 * chans, 6 * chans), jnp.bfloat16)] * 4,
        compiler_params=pltpu.CompilerParams(vmem_limit_bytes=60 * 1024 * 1024),
        name="network",
    )(levels, cond, noisy, row_ends, col_ends, w1, w2, wa, wb, b1, b2, ba, gain)


def local(
    members, strips, subs,
    noisy, condition, levels, enc_w1, enc_b1, enc_w2, enc_b2, den_wa, den_ba, noise_gain, den_wb
):
    field = jnp.transpose(noisy[0], (1, 2, 0))
    rows, cols, chans = field.shape
    inputs = condition.shape[0]
    cond = jnp.pad(jnp.transpose(condition, (1, 0, 2)), ((0, 0), (0, CH - inputs), (0, 0)))
    cond_all, row_ends, col_ends = exchange(cond, field, members, strips, subs)

    w1 = jnp.pad(enc_w1, ((0, 0), (0, 0), (0, CH - inputs))).reshape(3, 3, chans, CH)
    w1 = jnp.transpose(w1, (2, 1, 0, 3))
    w1 = jnp.concatenate([
        jnp.pad(w1, ((0, 0), (0, 0), (0, 1), (0, 0))),
        jnp.pad(w1, ((0, 0), (0, 0), (1, 0), (0, 0))),
    ], axis=0).reshape(2 * chans, 3, 2, 2 * CH)
    w1 = jnp.transpose(w1, (0, 2, 1, 3)).reshape(2 * chans, 12 * CH)

    out = network(strips, subs, levels, cond_all, field, row_ends, col_ends, w1, enc_w2, den_wa, den_wb,
                  enc_b1[None], enc_b2[None], den_ba[None], noise_gain[None])
    return jnp.transpose(out, (2, 0, 1))[None]


def solution(mesh):
    return jax.shard_map(
        functools.partial(local, mesh.shape["member"], mesh.shape["strip"], mesh.shape["sub"]),
        mesh=mesh,
        in_specs=(
            P(("group", "member"), None, "strip", "sub"),
            P("group", ("strip", "member"), "sub"),
            P(("group", "member")),
            P(), P(), P(), P(), P(), P(), P(), P(),
        ),
        out_specs=P(("group", "member"), None, "strip", "sub"),
        check_vma=False,
    )
```

time: 78.5 us -> 64 us (0.82)
  Pallas kernels: 63.6 us -> 51.6 us
  other arithmetic: 2.3 us -> 0.01 us
    pallas_call x1, Pallas kernels: 46.4 us -> 35.1 us  [network(): pl.pallas_call(functools.partial(network_kernel, strips, subs), out_shape...]
    broadcast_in_dim x1 -> x0, other arithmetic: 1.15 us -> none  [local(): offset_a = (den_ba + c_noise * noise_gain)[None]]
    another operation x2 -> x0, other arithmetic: 1.14 us -> none  [the longest x1 0.58 us: local(): jnp.stack([-strip * rows, (strips - strip) * rows, SIDE - sub * cols, SID...]
where the time goes in v1:
time: 64 us; the launch traced here: 63.6 us
  Pallas kernels  51.6 us (81%)
  local copies, waits for them, and re-layouts  11.3 us (18%)
  between operations  0.69 us (1%)
    pallas_call x1, Pallas kernels, network(): pl.pallas_call(functools.partial(network_kernel, strips, subs), out_shape...  35.1 us
    pallas_call x1, Pallas kernels, exchange(): pl.pallas_call(functools.partial(exchange_kernel, members, strips, subs),...  16.5 us
    unnamed x2, local copies, waits for them, and re-layouts  4.99 us
    broadcast_in_dim x1, local copies, waits for them, and re-layouts, local(): return jnp.transpose(out, (2, 0, 1))[None]  4.11 us

profile of v1, /device:TPU:0, one launch (start us, length us, event | category | flops | bytes accessed | tf_op | source)
XLA Modules:
  0.0 63.6 jit_solution(15097463553099298057)
XLA Ops:
  0.7 0.8 %pad.17 = bf16[9,128,16]{1,2,0:T(8,128)(2,1)S(1)} pad(bf16[9,128,12]{1,2,0:T(8,128)(2,1)} %param.14, bf16[]{:T(256)} %constant.2.clone.1), padding=0_0x0_0x0_4 | pad | bytes 64514 | tf_op jit(solution)/shard_map/jit(_pad)/pad | solution.py:333
  1.5 0.8 %copy.24.w1_ref = bf16[256,192]{1,0:T(8,128)(2,1)} copy(bf16[256,192]{0,1:T(8,128)(2,1)S(1)} %bitcast.24) | data formatting | bytes 196608 | tf_op jit(solution)/shard_map/reshape | solution.py:339
  2.3 0.8 %copy.27 = bf16[12,16,128]{2,0,1:T(8,128)(2,1)S(1)} copy(bf16[12,16,128]{2,1,0:T(8,128)(2,1)} %param.12) | data formatting | bytes 98304 | tf_op args[1]
  3.1 0.6 pad.16.cond_ref
  3.7 4.2 %copy.21 = bf16[1,128,64,128]{1,3,2,0:T(8,128)(2,1)} copy(bf16[1,128,64,128]{3,2,1,0:T(8,128)(2,1)} %param.11) | data formatting | bytes 4194304 | tf_op args[0]
  7.9 16.5 %exchange.1 = (bf16[72,16,384]{2,1,0:T(8,128)(2,1)}, bf16[2,2,144,128]{3,2,1,0:T(8,128)(2,1)}, bf16[2,64,8,128]{3,2,1,0:T(8,128)(2,1)}) custom-call(bf16[16,16,128]{2,1,0:T(8,128)(2,1)} %pad.16.cond_ref, bf16[64,128,128]{2,1,0:T(8,128)(2,1)} %bitcast.20), custom_call_target="tpu_custom_call" | custom-call | tf_op jit(solution)/shard_map/exchange/pallas_call | solution.py:124
  24.4 35.1 %network.1 = bf16[64,128,128]{2,1,0:T(8,128)(2,1)} custom-call(s32[1]{0:T(128)S(6)} %copy.28.levels, bf16[72,16,384]{2,1,0:T(8,128)(2,1)} %get-tuple-element.8.cond_ref, bf16[64,128,128]{2,1,0:T(8,128)(2,1)} %bitcast.21, bf16[2,2,144,128]{3,2,1,0:T(8,128)(2,1)} %get-tuple-element.9.rows_ref, bf16[2,64,8,128]{3,2,1,0:T(8,128)(2,1)} %get-tuple-element.10.cols_ref, ...), custom_call_target="tpu_custom_call" | custom-call | tf_op jit(solution)/shard_map/network/pallas_call | solution.py:310
  59.5 4.1 %copy.25 = bf16[1,128,64,128]{3,2,1,0:T(8,128)(2,1)} copy(bf16[1,128,64,128]{1,3,2,0:T(8,128)(2,1)} %bitcast.22) | data formatting | bytes 4194304 | tf_op jit(solution)/shard_map/broadcast_in_dim | solution.py:343
  (3 shorter events, 0.0 us)
